TPU v7x, 256 devices: a whole 4x4x8 slice. The times are simulated.
256 devices in a mesh: rows: 128 (over z, y, x), cols: 2 (over core).
Axes of the slice: x: 4, y: 4, z: 8, core: 2. Of those that a mesh axis runs over, the one named last changes fastest.
Arguments:
- design: float32 [131072, 512], P('rows', 'cols'), may hold values from -24 to 24
- signs: int32 [131072], P('rows'), may hold values from -1 to 1, as said below
- kept: int32 [8192], replicated, may hold values from 0 to 131071, as said below
Outputs:
- sketch: float32 [8192, 512], P('rows', 'cols')
- factor: float32 [512, 512], P(None, 'cols')
Inputs may be any that keep to these rules, and one draw needn't show every extreme that they name: `signs`: each entry is +1 or -1. `kept`: distinct and increasing.
All inputs are finite; a program needn't handle non-finite values.
Results may differ from a plain program's by a relative error of at most 0.0003.
Values sent between devices are 32-bit elements; how exact they have to be, the bound alone decides.
No kernel may reach another device: no remote copies, remote signals or barrier semaphores. Data moves between devices by JAX's collectives and lax.ppermute only.
A program may use at most 64 MiB of HBM per device.

v0:
```python
import math
import jax
import jax.numpy as jnp
from jax import lax
from jax.sharding import Mesh
from jax.sharding import PartitionSpec as P

ROWS = ("rows_0", "rows_1", "rows_2")


def sum_by_axis(so_far, axes):
    for axis in axes:
        so_far = lax.psum_scatter(so_far, axis, scatter_dimension=0, tiled=True)
    return so_far


def laid_out(parts, dim):
    dims = list(parts.shape[1:])
    dims[dim] *= parts.shape[0]
    return jnp.moveaxis(parts, 0, dim).reshape(dims)


def copy_for_each(shard, axis):
    length = lax.axis_size(axis)
    return lax.all_to_all(
        jnp.broadcast_to(shard[None], (length, *shard.shape)), axis, 0, 0, tiled=True
    )


def gathered_copies(shard, axis, dim):
    return laid_out(copy_for_each(shard, axis), dim)


def hadamard(order):
    matrix = jnp.ones((1, 1), jnp.float32)
    base = jnp.array([[1.0, 1.0], [1.0, -1.0]], jnp.float32)
    while matrix.shape[0] < order:
        matrix = jnp.kron(matrix, base)
    return matrix


def bit_parity(value):
    folded = value
    for amount in (16, 8, 4, 2, 1):
        folded = jnp.bitwise_xor(folded, jnp.right_shift(folded, amount))
    return jnp.bitwise_and(folded, 1)


def local_transform(flipped):
    length, width = flipped.shape
    outer = length // 128
    inner_table = hadamard(128)
    outer_table = hadamard(outer)
    blocks = flipped.reshape(outer, 128, width)
    mixed = jnp.einsum("pb,abc->apc", inner_table, blocks, precision=lax.Precision.HIGHEST)
    mixed = jnp.einsum("qa,apc->qpc", outer_table, mixed, precision=lax.Precision.HIGHEST)
    return mixed.reshape(length, width)


def signed_rows(transformed, kept_part, device_row, total_rows):
    length = transformed.shape[0]
    kept_blocks = kept_part // length
    offsets = kept_part - kept_blocks * length
    parity = bit_parity(jnp.bitwise_and(kept_blocks, device_row))
    factor = (1.0 - 2.0 * parity.astype(jnp.float32)) / math.sqrt(total_rows)
    return jnp.take(transformed, offsets, axis=0) * factor[:, None]


def body(design, signs, kept):
    flipped = design * signs.astype(jnp.float32)[:, None]
    transformed = local_transform(flipped)
    device_row = lax.axis_index(ROWS)
    groups = lax.axis_size(ROWS)
    length = transformed.shape[0]
    widths = transformed.shape[1]
    total_rows = length * groups
    sketch = sum_by_axis(signed_rows(transformed, kept, device_row, total_rows), ROWS)
    column = lax.axis_index("cols")
    whole = gathered_copies(sketch, "cols", 1)
    kept_total = kept.shape[0]
    partial_gram = jnp.dot(
        whole.T, whole, precision=lax.Precision.HIGHEST, preferred_element_type=jnp.float32
    )
    gram = lax.psum(partial_gram, ROWS) / kept_total
    factor = jnp.linalg.cholesky(gram).T
    return (sketch, lax.dynamic_slice_in_dim(factor, column * widths, widths, 1))


def solution(mesh):
    torus = Mesh(
        mesh.devices.reshape(8, 4, 4, mesh.shape["cols"]), ("rows_0", "rows_1", "rows_2", "cols")
    )
    return jax.shard_map(
        body,
        mesh=torus,
        in_specs=(P(ROWS, "cols"), P(ROWS), P()),
        out_specs=(P(ROWS, "cols"), P(None, "cols")),
        check_vma=False,
    )
```

profile of v0, /device:TPU:2, one launch (start us, length us, event | category | flops | bytes accessed | tf_op | source)
XLA Modules:
  0.0 540.0 jit_solution(2784497924892284188)
XLA Ops:
  7.2 0.8 broadcast_multiply_fusion.7
  8.1 0.1 mul.255
  8.2 0.8 broadcast_multiply_fusion.6
  9.1 0.8 broadcast_clamp_fusion
  9.9 0.8 compare_and_fusion
  10.7 0.7 convert_element_type.6
  11.4 0.8 broadcast_multiply_fusion.5
  12.2 0.8 broadcast_multiply_fusion.4
  13.0 0.1 mul.277
  13.1 0.9 broadcast_multiply_fusion.2
  14.0 0.6 mul.281
  14.7 3.0 broadcast_multiply_fusion
  17.7 4.0 reshape.195
  21.7 0.2 broadcast_multiply_fusion.3
  21.9 1.8 convolution_bitcast_fusion
  23.7 0.5 copy.15
  24.2 1.0 fusion.21
  25.2 0.3 copy.16
  25.6 31.4 %gather_fusion = f32[8192,256]{1,0:T(8,128)} fusion(f32[1024,256]{1,0:T(8,128)S(1)} %bitcast.45, s32[8192]{0:T(1024)S(1)} %broadcast_clamp_fusion), kind=kCustom, calls=%fused_computation | custom fusion | bytes 16809984 | tf_op jit(solution)/shard_map/jit(_take)/gather | solution.py:66
  57.0 9.9 %select_multiply_fusion = f32[8192,256]{1,0:T(8,128)} fusion(f32[8192,256]{1,0:T(8,128)} %gather_fusion, f32[8192]{0:T(1024)S(1)} %fusion.19, pred[8192]{0:T(1024)(128)(4,1)S(1)} %compare_and_fusion), kind=kLoop, calls=%fused_computation.1 | loop fusion | flops 4194304 | bytes 16818176 | tf_op jit(solution)/shard_map/mul | solution.py:66
  66.9 97.9 %reduce-scatter.4.cloned.1.call-done = f32[1024,256]{1,0:T(8,128)} async-done(((f32[8192,256]{1,0:T(8,128)}), f32[1024,256]{1,0:T(8,128)}) %reduce-scatter.4.cloned.1.call-update) | async-done | bytes 1048592 | tf_op jit(solution)/shard_map/reduce_scatter | solution.py:13
  165.0 27.3 %reduce-scatter.6.cloned.1.call-done = f32[256,256]{1,0:T(8,128)} async-done(((f32[1024,256]{1,0:T(8,128)}), f32[256,256]{1,0:T(8,128)}) %reduce-scatter.6.cloned.1.call-update) | async-done | bytes 262160 | tf_op jit(solution)/shard_map/reduce_scatter | solution.py:13
  192.3 24.3 %reduce-scatter.8.cloned.1.call-done = f32[64,256]{1,0:T(8,128)} async-done(((f32[256,256]{1,0:T(8,128)}), f32[64,256]{1,0:T(8,128)}) %reduce-scatter.8.cloned.1.call-update) | async-done | bytes 65552 | tf_op jit(solution)/shard_map/reduce_scatter | solution.py:13
  216.6 0.8 broadcast_in_dim.59
  217.4 3.8 all_to_all.5
  221.3 2.1 fusion.22
  223.4 222.7 %all-reduce.3.cloned.1.call-done = f32[512,512]{0,1:T(8,128)} async-done(((f32[512,512]{0,1:T(8,128)}), f32[512,512]{0,1:T(8,128)}) %all-reduce.3.cloned.1.call-update) | async-done | bytes 1048592 | tf_op jit(solution)/shard_map/psum | solution.py:84
  446.1 1.3 broadcast_multiply_fusion.1
  447.4 0.3 copy.19
  447.7 1.5 fusion
  449.2 11.7 %cholesky.104 = f32[128,128]{1,0:T(8,128)S(1)} custom-call(f32[128,128]{1,0:T(8,128)S(1)} %cholesky.266), custom_call_target="Cholesky" | custom-call | tf_op jit(solution)/shard_map/jit(cholesky)/cholesky | solution.py:85
  461.0 0.1 cholesky.224
  461.1 9.8 %custom-call.27 = f32[1,128,128]{1,2,0:T(8,128)S(1)} custom-call(f32[1,128,128]{2,1,0:T(8,128)S(1)} %get-tuple-element.17), custom_call_target="InvertDiagBlocksLowerTriangular" | custom-call | tf_op jit(solution)/shard_map/jit(cholesky)/cholesky | solution.py:85
  470.9 0.3 constant_dynamic-update-slice_fusion.1
  471.2 0.3 convolution_subtract_fusion
  471.6 11.7 %cholesky.217 = f32[128,128]{1,0:T(8,128)S(1)} custom-call(f32[128,128]{1,0:T(8,128)S(1)} %cholesky.270), custom_call_target="Cholesky" | custom-call | tf_op jit(solution)/shard_map/jit(cholesky)/cholesky | solution.py:85
  483.3 9.9 %custom-call.28 = f32[1,128,128]{1,2,0:T(8,128)S(1)} custom-call(f32[1,128,128]{2,1,0:T(8,128)S(1)} %get-tuple-element.14), custom_call_target="InvertDiagBlocksLowerTriangular" | custom-call | tf_op jit(solution)/shard_map/jit(cholesky)/cholesky | solution.py:85
  493.3 0.3 convolution_dynamic-update-slice_fusion
  493.6 0.4 convolution_subtract_fusion.1
  494.0 11.7 %cholesky.238 = f32[128,128]{1,0:T(8,128)S(1)} custom-call(f32[128,128]{1,0:T(8,128)S(1)} %cholesky.275), custom_call_target="Cholesky" | custom-call | tf_op jit(solution)/shard_map/jit(cholesky)/cholesky | solution.py:85
  505.7 9.8 %custom-call.29 = f32[1,128,128]{1,2,0:T(8,128)S(1)} custom-call(f32[1,128,128]{2,1,0:T(8,128)S(1)} %get-tuple-element.11), custom_call_target="InvertDiagBlocksLowerTriangular" | custom-call | tf_op jit(solution)/shard_map/jit(cholesky)/cholesky | solution.py:85
  515.5 0.2 convolution_dynamic-update-slice_fusion.1
  515.7 0.4 convolution_subtract_fusion.2
  516.1 11.7 %cholesky.255 = f32[128,128]{1,0:T(8,128)S(1)} custom-call(f32[128,128]{1,0:T(8,128)S(1)} %convolution_subtract_fusion.2), custom_call_target="Cholesky" | custom-call | tf_op jit(solution)/shard_map/jit(cholesky)/cholesky | solution.py:85
  527.9 0.7 compare_reduce_fusion.1
  528.6 0.6 compare_reduce_fusion
  529.2 0.7 compare_reduce_fusion.2
  532.5 1.0 copy.20
  (25 shorter events, 0.8 us)
Async XLA Ops:
  7.2 14.5 %copy-start = (f32[1024,256]{1,0:T(8,128)S(1)}, f32[1024,256]{1,0:T(8,128)}, u32[]{:S(2)}) copy-start(f32[1024,256]{1,0:T(8,128)} %param.5) | copy-start | bytes 3145732
  7.2 157.7 %reduce-scatter.4.cloned.1.call-start = ((), (), s32[]{:S(2)}) async-start(), calls=%async_computation.4 | async-start | bytes 9437184 | tf_op jit(solution)/shard_map/reduce_scatter | solution.py:13
  17.7 7.9 %copy-start.1 = (s32[8192]{0:T(1024)S(1)}, s32[8192]{0:T(1024)}, u32[]{:S(2)}) copy-start(s32[8192]{0:T(1024)} %param.7) | copy-start | bytes 98308
  66.9 125.3 %reduce-scatter.6.cloned.1.call-start = ((), (), s32[]{:S(2)}) async-start(), calls=%async_computation.5 | async-start | bytes 1310720 | tf_op jit(solution)/shard_map/reduce_scatter | solution.py:13
  164.9 51.7 %reduce-scatter.8.cloned.1.call-start = ((), (), s32[]{:S(2)}) async-start(), calls=%async_computation.6 | async-start | bytes 327680 | tf_op jit(solution)/shard_map/reduce_scatter | solution.py:13
  192.3 253.8 %all-reduce.3.cloned.1.call-start = ((), (), s32[]{:S(2)}) async-start(), calls=%async_computation.7 | async-start | bytes 2097152 | tf_op jit(solution)/shard_map/psum | solution.py:84
Sparse Core Ops, SparseCore 0:
  67.0 97.8 reduce-scatter.3
  167.4 24.7 reduce-scatter.5
  195.5 21.0 reduce-scatter.7
  223.5 222.5 all-reduce.2
where the time goes:
time: 541 us; the launch traced here: 540 us
  waiting for transfers between devices  372 us (69%)
  other arithmetic  101 us (19%)
  local copies, waits for them, and re-layouts  39.6 us (7%)
  between operations  16.6 us (3%)
  matrix products  6.71 us (1%)
    psum x1, waiting for transfers between devices, body(): gram = lax.psum(partial_gram, ROWS) / kept_total  223 us
    reduce_scatter x3, waiting for transfers between devices, sum_by_axis(): so_far = lax.psum_scatter(so_far, axis, scatter_dimension=0, tiled=True)  149 us
    another operation x14, other arithmetic, body(): factor = jnp.linalg.cholesky(gram).T  78.6 us
    gather x1, local copies, waits for them, and re-layouts, signed_rows(): return jnp.take(transformed, offsets, axis=0) * factor[:, None]  31.4 us
  transfers between devices with their start and end apart: 4, of which 4 were waited for; matrix products, arithmetic and copies ran while one was open for 0% of the time, Pallas kernels for 0%

commit v1 on v0

--- a/solution.py
+++ b/solution.py
@@ -6,6 +6,11 @@
 from jax.sharding import PartitionSpec as P
 
 ROWS = ("rows_0", "rows_1", "rows_2")
+
+
+def axis_by_axis(x, axis_one, axis_two):
+    partial = lax.psum(x, axis_one)
+    return lax.psum(partial, axis_two)
 
 
 def sum_by_axis(so_far, axes):
@@ -81,7 +86,7 @@
     partial_gram = jnp.dot(
         whole.T, whole, precision=lax.Precision.HIGHEST, preferred_element_type=jnp.float32
     )
-    gram = lax.psum(partial_gram, ROWS) / kept_total
+    gram = axis_by_axis(partial_gram, "rows_0", ("rows_1", "rows_2")) / kept_total
     factor = jnp.linalg.cholesky(gram).T
     return (sketch, lax.dynamic_slice_in_dim(factor, column * widths, widths, 1))
 

time: 541 us -> 494 us (0.913)
  waiting for transfers between devices: 372 us -> 325 us
    psum x1 -> x2, waiting for transfers between devices: 223 us -> 175 us  [the longest x1 98.1 us: axis_by_axis(): return lax.psum(partial, axis_two)]
  transfers between devices with their start and end apart: 4 -> 5, of which waited for: 4 -> 5; matrix products, arithmetic and copies ran while one was open for 0% -> 0% of each run, Pallas kernels for 0% -> 0%
where the time goes in v1:
time: 494 us; the launch traced here: 493 us
  waiting for transfers between devices  325 us (66%)
  other arithmetic  101 us (20%)
  local copies, waits for them, and re-layouts  39.6 us (8%)
  between operations  16.6 us (3%)
  matrix products  6.7 us (1%)
    reduce_scatter x3, waiting for transfers between devices, sum_by_axis(): so_far = lax.psum_scatter(so_far, axis, scatter_dimension=0, tiled=True)  149 us
    psum x1, waiting for transfers between devices, axis_by_axis(): return lax.psum(partial, axis_two)  98.1 us
    another operation x14, other arithmetic, body(): factor = jnp.linalg.cholesky(gram).T  78.6 us
    psum x1, waiting for transfers between devices, axis_by_axis(): partial = lax.psum(x, axis_one)  77.4 us
    gather x1, local copies, waits for them, and re-layouts, signed_rows(): return jnp.take(transformed, offsets, axis=0) * factor[:, None]  31.4 us
    mul x1, other arithmetic, signed_rows(): return jnp.take(transformed, offsets, axis=0) * factor[:, None]  9.89 us
  transfers between devices with their start and end apart: 5, of which 5 were waited for; matrix products, arithmetic and copies ran while one was open for 0% of the time, Pallas kernels for 0%

profile of v1, /device:TPU:2, one launch (start us, length us, event | category | flops | bytes accessed | tf_op | source)
XLA Modules:
  0.0 493.1 jit_solution(16199066192971871080)
XLA Ops:
  7.2 0.8 broadcast_multiply_fusion.7
  8.2 0.8 broadcast_multiply_fusion.6
  9.1 0.8 broadcast_clamp_fusion
  9.9 0.8 compare_and_fusion
  10.7 0.7 convert_element_type.6
  11.4 0.8 broadcast_multiply_fusion.5
  12.2 0.8 broadcast_multiply_fusion.4
  13.0 0.1 mul.277
  13.1 0.9 broadcast_multiply_fusion.2
  14.0 0.6 mul.281
  14.7 3.0 broadcast_multiply_fusion
  17.7 4.0 reshape.195
  21.7 0.2 broadcast_multiply_fusion.3
  21.9 1.8 convolution_bitcast_fusion
  23.7 0.5 copy.15
  24.2 1.0 fusion.21
  25.2 0.3 copy.16
  25.6 31.4 %gather_fusion = f32[8192,256]{1,0:T(8,128)} fusion(f32[1024,256]{1,0:T(8,128)S(1)} %bitcast.45, s32[8192]{0:T(1024)S(1)} %broadcast_clamp_fusion), kind=kCustom, calls=%fused_computation | custom fusion | bytes 16809984 | tf_op jit(solution)/shard_map/jit(_take)/gather | solution.py:71
  57.0 9.9 %select_multiply_fusion = f32[8192,256]{1,0:T(8,128)} fusion(f32[8192,256]{1,0:T(8,128)} %gather_fusion, f32[8192]{0:T(1024)S(1)} %fusion.19, pred[8192]{0:T(1024)(128)(4,1)S(1)} %compare_and_fusion), kind=kLoop, calls=%fused_computation.1 | loop fusion | flops 4194304 | bytes 16818176 | tf_op jit(solution)/shard_map/mul | solution.py:71
  66.9 97.9 %reduce-scatter.4.cloned.1.call-done = f32[1024,256]{1,0:T(8,128)} async-done(((f32[8192,256]{1,0:T(8,128)}), f32[1024,256]{1,0:T(8,128)}) %reduce-scatter.4.cloned.1.call-update) | async-done | bytes 1048592 | tf_op jit(solution)/shard_map/reduce_scatter | solution.py:18
  165.0 27.3 %reduce-scatter.6.cloned.1.call-done = f32[256,256]{1,0:T(8,128)} async-done(((f32[1024,256]{1,0:T(8,128)}), f32[256,256]{1,0:T(8,128)}) %reduce-scatter.6.cloned.1.call-update) | async-done | bytes 262160 | tf_op jit(solution)/shard_map/reduce_scatter | solution.py:18
  192.3 24.3 %reduce-scatter.8.cloned.1.call-done = f32[64,256]{1,0:T(8,128)} async-done(((f32[256,256]{1,0:T(8,128)}), f32[64,256]{1,0:T(8,128)}) %reduce-scatter.8.cloned.1.call-update) | async-done | bytes 65552 | tf_op jit(solution)/shard_map/reduce_scatter | solution.py:18
  216.6 0.8 broadcast_in_dim.59
  217.4 3.8 all_to_all.5
  221.3 2.1 fusion.22
  223.4 0.2 all-reduce.6.cloned.1.call-start
  223.6 77.4 %all-reduce.4.cloned.1.call-done = f32[512,512]{0,1:T(8,128)} async-done(((f32[512,512]{0,1:T(8,128)}), f32[512,512]{0,1:T(8,128)}) %all-reduce.4.cloned.1.call-update) | async-done | bytes 1048592 | tf_op jit(solution)/shard_map/psum | solution.py:12
  301.0 98.1 %all-reduce.6.cloned.1.call-done = f32[512,512]{0,1:T(8,128)} async-done(((f32[512,512]{0,1:T(8,128)}), f32[512,512]{0,1:T(8,128)}) %all-reduce.6.cloned.1.call-update) | async-done | bytes 1048592 | tf_op jit(solution)/shard_map/psum | solution.py:13
  399.1 1.3 broadcast_multiply_fusion.1
  400.4 0.3 copy.19
  400.8 1.5 fusion
  402.2 11.7 %cholesky.104 = f32[128,128]{1,0:T(8,128)S(1)} custom-call(f32[128,128]{1,0:T(8,128)S(1)} %cholesky.266), custom_call_target="Cholesky" | custom-call | tf_op jit(solution)/shard_map/jit(cholesky)/cholesky | solution.py:90
  414.1 9.8 %custom-call.27 = f32[1,128,128]{1,2,0:T(8,128)S(1)} custom-call(f32[1,128,128]{2,1,0:T(8,128)S(1)} %get-tuple-element.17), custom_call_target="InvertDiagBlocksLowerTriangular" | custom-call | tf_op jit(solution)/shard_map/jit(cholesky)/cholesky | solution.py:90
  423.9 0.3 constant_dynamic-update-slice_fusion.1
  424.3 0.3 convolution_subtract_fusion
  424.6 11.7 %cholesky.217 = f32[128,128]{1,0:T(8,128)S(1)} custom-call(f32[128,128]{1,0:T(8,128)S(1)} %cholesky.270), custom_call_target="Cholesky" | custom-call | tf_op jit(solution)/shard_map/jit(cholesky)/cholesky | solution.py:90
  436.4 10.0 %custom-call.28 = f32[1,128,128]{1,2,0:T(8,128)S(1)} custom-call(f32[1,128,128]{2,1,0:T(8,128)S(1)} %get-tuple-element.14), custom_call_target="InvertDiagBlocksLowerTriangular" | custom-call | tf_op jit(solution)/shard_map/jit(cholesky)/cholesky | solution.py:90
  446.4 0.3 convolution_dynamic-update-slice_fusion
  446.6 0.4 convolution_subtract_fusion.1
  447.0 11.7 %cholesky.238 = f32[128,128]{1,0:T(8,128)S(1)} custom-call(f32[128,128]{1,0:T(8,128)S(1)} %cholesky.275), custom_call_target="Cholesky" | custom-call | tf_op jit(solution)/shard_map/jit(cholesky)/cholesky | solution.py:90
  458.8 9.8 %custom-call.29 = f32[1,128,128]{1,2,0:T(8,128)S(1)} custom-call(f32[1,128,128]{2,1,0:T(8,128)S(1)} %get-tuple-element.11), custom_call_target="InvertDiagBlocksLowerTriangular" | custom-call | tf_op jit(solution)/shard_map/jit(cholesky)/cholesky | solution.py:90
  468.6 0.2 convolution_dynamic-update-slice_fusion.1
  468.8 0.4 convolution_subtract_fusion.2
  469.2 11.7 %cholesky.255 = f32[128,128]{1,0:T(8,128)S(1)} custom-call(f32[128,128]{1,0:T(8,128)S(1)} %convolution_subtract_fusion.2), custom_call_target="Cholesky" | custom-call | tf_op jit(solution)/shard_map/jit(cholesky)/cholesky | solution.py:90
  480.9 0.7 compare_reduce_fusion.1
  481.7 0.6 compare_reduce_fusion
  482.3 0.7 compare_reduce_fusion.2
  485.6 1.0 copy.20
  (28 shorter events, 1.0 us)
Async XLA Ops:
  7.2 14.5 %copy-start = (f32[1024,256]{1,0:T(8,128)S(1)}, f32[1024,256]{1,0:T(8,128)}, u32[]{:S(2)}) copy-start(f32[1024,256]{1,0:T(8,128)} %param.5) | copy-start | bytes 3145732
  7.2 157.7 %reduce-scatter.4.cloned.1.call-start = ((), (), s32[]{:S(2)}) async-start(), calls=%async_computation.4 | async-start | bytes 9437184 | tf_op jit(solution)/shard_map/reduce_scatter | solution.py:18
  17.7 7.9 %copy-start.1 = (s32[8192]{0:T(1024)S(1)}, s32[8192]{0:T(1024)}, u32[]{:S(2)}) copy-start(s32[8192]{0:T(1024)} %param.7) | copy-start | bytes 98308
  66.9 125.3 %reduce-scatter.6.cloned.1.call-start = ((), (), s32[]{:S(2)}) async-start(), calls=%async_computation.5 | async-start | bytes 1310720 | tf_op jit(solution)/shard_map/reduce_scatter | solution.py:18
  164.9 51.7 %reduce-scatter.8.cloned.1.call-start = ((), (), s32[]{:S(2)}) async-start(), calls=%async_computation.6 | async-start | bytes 327680 | tf_op jit(solution)/shard_map/reduce_scatter | solution.py:18
  192.3 108.7 %all-reduce.4.cloned.1.call-start = ((), (), s32[]{:S(2)}) async-start(), calls=%async_computation.7 | async-start | bytes 2097152 | tf_op jit(solution)/shard_map/psum | solution.py:12
  223.4 175.7 %all-reduce.6.cloned.1.call-start = ((), (), s32[]{:S(2)}) async-start(), calls=%async_computation.8 | async-start | bytes 2097152 | tf_op jit(solution)/shard_map/psum | solution.py:13
Sparse Core Ops, SparseCore 0:
  67.0 97.8 reduce-scatter.3
  167.4 24.7 reduce-scatter.5
  195.5 21.0 reduce-scatter.7
  223.5 77.4 all-reduce.3
  304.1 94.9 all-reduce.5
